TPU v7x, 256 devices: a whole 4x4x8 slice. The times are simulated.
256 devices in a mesh: bead: 8 (over y_lo, x), dom: 32 (over y_hi, z, core).
Axes of the slice: x: 4, y: 4 (y_hi: 2, y_lo: 2; y = y_hi * 2 + y_lo), z: 8, core: 2. Of those that a mesh axis runs over, the one named last changes fastest.
Arguments:
- mode_pos: float32 [16, 3, 24576], P('bead', None, 'dom'), may hold values from -6 to 6
- mode_vel: float32 [16, 3, 24576], P('bead', None, 'dom'), may hold values from -6 to 6
- charges: float32 [24576], P('dom'), may hold values from -1.5 to 1.5
Outputs:
- positions: float32 [16, 3, 24576], P('bead', None, 'dom')
- velocities: float32 [16, 3, 24576], P('bead', None, 'dom')
All inputs are finite; a program needn't handle non-finite values.
Results may differ from a plain program's by a relative error of at most 0.0003.
Values sent between devices are 32-bit elements; how exact they have to be, the bound alone decides.
No kernel may reach another device: no remote copies, remote signals or barrier semaphores. Data moves between devices by JAX's collectives and lax.ppermute only.
A program may use at most 64 MiB of HBM per device.

v0:
```python
import jax
import jax.numpy as jnp
from jax import lax
from jax.sharding import PartitionSpec as P

BEADS = 16
KAPPA = 2.0
SOFTEN = 0.09
KICK = 0.3
OMEGA = 7.0
STEP_TIME = 0.1
HIGHEST = lax.Precision.HIGHEST


def mode_table(bead_index, mode_index):
    scale_root = jnp.sqrt(jnp.float32(BEADS))
    angle = 2.0 * jnp.pi * bead_index.astype(jnp.float32) * mode_index.astype(jnp.float32) / BEADS
    first = jnp.ones_like(angle) / scale_root
    middle = jnp.cos(jnp.pi * bead_index.astype(jnp.float32)) / scale_root + 0.0 * angle
    factor = jnp.sqrt(2.0 / jnp.float32(BEADS))
    return jnp.where(
        mode_index == 0,
        first,
        jnp.where(
            2 * mode_index < BEADS,
            factor * jnp.cos(angle),
            jnp.where(2 * mode_index == BEADS, middle, factor * jnp.sin(angle)),
        ),
    )


def evolve(mode_pos, mode_vel, mode_index):
    freq = 2.0 * OMEGA * jnp.sin(jnp.pi * mode_index.astype(jnp.float32) / BEADS)
    theta = freq * STEP_TIME
    cosine = jnp.cos(theta)[:, None, None]
    sine = jnp.sin(theta)
    safe_freq = jnp.where(mode_index > 0, freq, 1.0)
    carry_rate = jnp.where(mode_index > 0, sine / safe_freq, STEP_TIME)[:, None, None]
    new_pos = cosine * mode_pos + carry_rate * mode_vel
    new_vel = (-freq * sine)[:, None, None] * mode_pos + cosine * mode_vel
    return (new_pos, new_vel)


def pair_block(near_pos, near_charge, far_pack):
    far_pos = far_pack[:, :3]
    far_charge = far_pack[:, 3]
    delta = near_pos[:, :, :, None] - far_pos[:, :, None, :]
    square = jnp.sum(delta * delta, axis=1) + SOFTEN
    distance = jnp.sqrt(square)
    weight = (
        near_charge[None, :, None]
        * far_charge[:, None, :]
        * jnp.exp(-KAPPA * distance)
        * (1.0 + KAPPA * distance)
        / (square * distance)
    )
    terms = weight[:, None] * delta
    return (jnp.sum(terms, axis=3), -jnp.sum(terms, axis=2))


def block_force(near_pos, near_charge, far_pack):
    far_count = far_pack.shape[2]
    span_size = far_count
    while span_size > 512 and span_size % 2 == 0:
        span_size = span_size // 2

    def one_span(total, span_index):
        piece = lax.dynamic_slice_in_dim(far_pack, span_index * span_size, span_size, 2)
        force_part, react_part = pair_block(near_pos, near_charge, piece)
        return (total + force_part, None)

    total, reacts = lax.scan(
        one_span, jnp.zeros_like(near_pos), jnp.arange(far_count // span_size, dtype=jnp.int32)
    )
    return (total, reacts)


def local(mode_pos, mode_vel, charges):
    local_beads = mode_pos.shape[0]
    own_modes = lax.axis_index("bead") * local_beads + jnp.arange(local_beads, dtype=jnp.int32)
    new_pos, new_vel = evolve(mode_pos, mode_vel, own_modes)
    pieces = (
        lax.all_gather(new_pos, "bead", axis=0, tiled=True),
        lax.all_gather(new_vel, "bead", axis=0, tiled=True),
    )
    span_count = pieces[0].shape[0]
    columns = jnp.arange(span_count, dtype=jnp.int32)
    table = mode_table(own_modes[:, None], columns[None, :])
    first = jnp.einsum("bk,kcn->bcn", table, pieces[0], precision=HIGHEST)
    second = jnp.einsum("bk,kcn->bcn", table, pieces[1], precision=HIGHEST)
    charge_rows = jnp.broadcast_to(charges[None, None, :], (local_beads, 1, charges.shape[0]))
    packed = jnp.concatenate((first, charge_rows), axis=1)
    force_part, unused = block_force(
        first, charges, lax.all_gather(packed, "dom", axis=2, tiled=True)
    )
    return (first, second + KICK * force_part)


def solution(mesh):
    placed = (P("bead", None, "dom"), P("bead", None, "dom"), P("dom"))
    return jax.shard_map(
        local,
        mesh=mesh,
        in_specs=placed,
        out_specs=(P("bead", None, "dom"), P("bead", None, "dom")),
        check_vma=False,
    )
```

profile of v0, /device:TPU:6, one launch (start us, length us, event | category | flops | bytes accessed | tf_op | source)
XLA Modules:
  0.0 468.5 jit_solution(9863614057664356881)
XLA Ops:
  1.6 28.3 %all_gather.9 = f32[16,3,768]{2,1,0:T(4,128)S(1)} all-gather(f32[2,3,768]{2,1,0:T(4,128)S(1)} %get-tuple-element.87), channel_id=1, replica_groups=mesh['bead'=8,'dom'=32] {'bead'}, dimensions={0}, use_global_device_ids=true | all-gather | bytes 165888 | tf_op jit(solution)/shard_map/all_gather | solution.py:83
  31.0 47.0 %all_gather.11 = f32[2,4,24576]{2,0,1:T(2,128)S(1)} all-gather(f32[2,4,768]{2,0,1:T(2,128)S(1)} %pad_maximum_fusion), channel_id=1, replica_groups=mesh['bead'=8,'dom'=32] {'dom'}, dimensions={2}, use_global_device_ids=true | all-gather | bytes 811008 | tf_op jit(solution)/shard_map/all_gather | solution.py:94
  78.1 361.2 %while.11 = (s32[]{:T(128)}, f32[2,3,768]{2,1,0:T(4,128)S(1)}, f32[768]{0:T(1024)}, s32[64]{0:T(128)S(1)}, f32[2,4,24576]{2,0,1:T(2,128)S(1)}, /*index=5*/f32[2,...) while((s32[]{:T(128)}, f32[2,3,768]{2,1,0:T(4,128)S(1)}, ...), condition=%wide.region_3.4_spmd.clone, body=%wide.region_0.3_spmd.clone.sunk | while | flops 15340040 | bytes 9627877 | solution.py:72
  80.5 1.7 fusion.30
  86.1 1.7 fusion.30
  103.0 1.7 fusion.30
  108.7 1.7 fusion.30
  114.3 1.7 fusion.30
  125.6 1.7 fusion.30
  131.3 1.7 fusion.30
  136.9 1.7 fusion.30
  142.5 1.7 fusion.30
  153.8 1.7 fusion.30
  159.5 1.7 fusion.30
  165.1 1.7 fusion.30
  170.8 1.7 fusion.30
  182.0 1.7 fusion.30
  187.7 1.7 fusion.30
  193.3 1.7 fusion.30
  210.3 1.7 fusion.30
  215.9 1.7 fusion.30
  221.6 1.7 fusion.30
  232.8 1.7 fusion.30
  238.5 1.7 fusion.30
  244.1 1.7 fusion.30
  249.8 1.7 fusion.30
  261.1 1.7 fusion.30
  266.7 1.7 fusion.30
  272.3 1.7 fusion.30
  278.0 1.7 fusion.30
  289.3 1.7 fusion.30
  439.3 28.3 %all_gather.10 = f32[16,3,768]{2,1,0:T(4,128)S(1)} all-gather(f32[2,3,768]{2,1,0:T(4,128)S(1)} %get-tuple-element.86), channel_id=1, replica_groups=mesh['bead'=8,'dom'=32] {'bead'}, dimensions={0}, use_global_device_ids=true | all-gather | bytes 165888 | tf_op jit(solution)/shard_map/all_gather | solution.py:84
  (628 shorter events, 270.5 us)
Async XLA Ops:
  30.3 47.8 %copy-start = (f32[2,3,768]{2,0,1:T(2,128)}, f32[2,3,768]{2,0,1:T(2,128)S(1)}, u32[]{:S(2)}) copy-start(f32[2,3,768]{2,0,1:T(2,128)S(1)} %fusion.8) | copy-start | bytes 55300
  78.1 2.4 copy-start.1
  83.7 2.4 copy-start.1
  89.4 2.4 copy-start.1
  95.0 2.4 copy-start.1
  100.7 2.4 copy-start.1
  106.3 2.4 copy-start.1
  112.0 2.4 copy-start.1
  117.6 2.4 copy-start.1
  123.2 2.4 copy-start.1
  128.9 2.4 copy-start.1
  134.5 2.4 copy-start.1
  140.2 2.4 copy-start.1
  162.7 2.4 copy-start.1
  168.4 2.4 copy-start.1
  191.0 2.4 copy-start.1
  196.6 2.4 copy-start.1
  219.2 2.4 copy-start.1
  224.8 2.4 copy-start.1
  247.4 2.4 copy-start.1
  270.0 2.4 copy-start.1
  275.6 2.4 copy-start.1
  298.2 2.4 copy-start.1
  303.8 2.4 copy-start.1
  326.4 2.4 copy-start.1
  332.1 2.4 copy-start.1
  354.6 2.4 copy-start.1
  377.2 2.4 copy-start.1
  382.9 2.4 copy-start.1
  405.4 2.4 copy-start.1
  411.1 2.4 copy-start.1
  433.6 2.4 copy-start.1
  (33 other events, 77.8 us)
where the time goes:
time: 469 us; the launch traced here: 468 us
  other arithmetic  274 us (58%)
  blocking collectives  104 us (22%)
  loops' own time  46.5 us (10%)
  local copies, waits for them, and re-layouts  42.1 us (9%)
    div x64, other arithmetic, pair_block(): near_charge[None, :, None] * far_charge[:, None, :]  108 us
    reduce_sum x64, other arithmetic, pair_block(): return (jnp.sum(terms, axis=3), -jnp.sum(terms, axis=2))  98.3 us
    reduce_sum x64, other arithmetic, pair_block(): square = jnp.sum(delta * delta, axis=1) + SOFTEN  65.7 us
    all_gather x1, blocking collectives, local(): lax.all_gather(packed, 'dom', axis=2, tiled=True)  47 us
    another operation x1, loops' own time, block_force(): lax.scan(one_span, jnp.zeros_like(near_pos), jnp.arange(far_count // span...  46.5 us
    dynamic_slice x64, local copies, waits for them, and re-layouts, block_force(): lax.scan(one_span, jnp.zeros_like(near_pos), jnp.arange(far_count // span...  39.2 us
    all_gather x1, blocking collectives, local(): lax.all_gather(new_vel, 'bead', axis=0, tiled=True)  28.3 us
    all_gather x1, blocking collectives, local(): lax.all_gather(new_pos, 'bead', axis=0, tiled=True)  28.3 us

commit v1 on v0

--- a/solution.py
+++ b/solution.py
@@ -91,7 +91,11 @@
     charge_rows = jnp.broadcast_to(charges[None, None, :], (local_beads, 1, charges.shape[0]))
     packed = jnp.concatenate((first, charge_rows), axis=1)
     force_part, unused = block_force(
-        first, charges, lax.all_gather(packed, "dom", axis=2, tiled=True)
+        first,
+        charges,
+        jnp.concatenate(
+            lax.all_to_all(jnp.stack([packed] * lax.axis_size("dom")), "dom", 0, 0), axis=2
+        ),
     )
     return (first, second + KICK * force_part)
 

time: 469 us -> 433 us (0.923)
  blocking collectives: 104 us -> 56.9 us
  starting transfers between devices: 0 us -> 11.6 us
    all_gather x1 -> x0, blocking collectives: 47 us -> none  [local(): lax.all_gather(packed, 'dom', axis=2, tiled=True)]
    all_to_all x0 -> x1, starting transfers between devices: none -> 11.6 us  [local(): lax.all_to_all(jnp.stack([packed] * lax.axis_size('dom')), 'dom', 0, 0)]
  transfers between devices with their start and end apart: 0 -> 1, of which waited for: 0 -> 0; matrix products, arithmetic and copies ran while one was open for 0% -> 0% of each run, Pallas kernels for 0% -> 0%
where the time goes in v1:
time: 433 us; the launch traced here: 432 us
  other arithmetic  274 us (63%)
  blocking collectives  56.9 us (13%)
  loops' own time  43.8 us (10%)
  local copies, waits for them, and re-layouts  43.6 us (10%)
  starting transfers between devices  11.6 us (3%)
    div x64, other arithmetic, pair_block(): near_charge[None, :, None] * far_charge[:, None, :]  108 us
    reduce_sum x64, other arithmetic, pair_block(): return (jnp.sum(terms, axis=3), -jnp.sum(terms, axis=2))  98.3 us
    reduce_sum x64, other arithmetic, pair_block(): square = jnp.sum(delta * delta, axis=1) + SOFTEN  65.7 us
    another operation x1, loops' own time, block_force(): lax.scan(one_span, jnp.zeros_like(near_pos), jnp.arange(far_count // span...  43.8 us
    dynamic_slice x64, local copies, waits for them, and re-layouts, block_force(): lax.scan(one_span, jnp.zeros_like(near_pos), jnp.arange(far_count // span...  39.5 us
    all_gather x1, blocking collectives, local(): lax.all_gather(new_vel, 'bead', axis=0, tiled=True)  28.7 us
    all_gather x1, blocking collectives, local(): lax.all_gather(new_pos, 'bead', axis=0, tiled=True)  28.3 us
    all_to_all x1, starting transfers between devices, local(): lax.all_to_all(jnp.stack([packed] * lax.axis_size('dom')), 'dom', 0, 0)  11.6 us
  transfers between devices with their start and end apart: 1, of which 0 were waited for; matrix products, arithmetic and copies ran while one was open for 0% of the time, Pallas kernels for 0%

profile of v1, /device:TPU:6, one launch (start us, length us, event | category | flops | bytes accessed | tf_op | source)
XLA Modules:
  0.0 432.3 jit_solution(1204356481395643995)
XLA Ops:
  1.7 28.3 %all_gather.6 = f32[16,3,768]{2,1,0:T(4,128)S(1)} all-gather(f32[2,3,768]{2,1,0:T(4,128)S(1)} %get-tuple-element.93), channel_id=1, replica_groups=mesh['bead'=8,'dom'=32] {'bead'}, dimensions={0}, use_global_device_ids=true | all-gather | bytes 165888 | tf_op jit(solution)/shard_map/all_gather | solution.py:83
  32.1 11.6 %all-to-all-start = ((f32[32,2,4,768]{3,2,1,0:T(4,128)}), f32[32,2,4,768]{3,2,1,0:T(4,128)S(1)}, u32[]{:S(2)}, u32[]{:S(2)}) async-start(f32[32,2,4,768]{3,2,1,0:T(4,128)} %stack.2), calls=%async_computation | async-start | bytes 1572864 | tf_op jit(solution)/shard_map/all_to_all | solution.py:97
  43.7 28.7 %all_gather.7 = f32[16,3,768]{2,1,0:T(4,128)S(1)} all-gather(f32[2,3,768]{2,1,0:T(4,128)S(1)} %get-tuple-element.92), channel_id=1, replica_groups=mesh['bead'=8,'dom'=32] {'bead'}, dimensions={0}, use_global_device_ids=true | all-gather | bytes 165888 | tf_op jit(solution)/shard_map/all_gather | solution.py:84
  73.2 358.2 %while.11 = (s32[]{:T(128)}, f32[2,3,768]{2,1,0:T(4,128)S(1)}, f32[768]{0:T(1024)S(1)}, s32[64]{0:T(128)S(1)}, f32[2,4,24576]{2,0,1:T(2,128)S(1)}, /*index=5*/f3...) while((s32[]{:T(128)}, f32[2,3,768]{2,1,0:T(4,128)S(1)}, ...), condition=%wide.region_3.4_spmd.clone, body=%wide.region_0.3_spmd.clone.sunk | while | flops 15340040 | bytes 9615561 | solution.py:72
  75.6 1.7 fusion.30
  97.9 1.7 fusion.30
  103.5 1.7 fusion.30
  109.1 1.7 fusion.30
  114.7 1.7 fusion.30
  120.3 1.7 fusion.30
  125.9 1.7 fusion.30
  131.5 1.7 fusion.30
  148.3 1.7 fusion.30
  153.9 1.7 fusion.30
  159.5 1.7 fusion.30
  165.1 1.7 fusion.30
  170.7 1.7 fusion.30
  176.3 1.7 fusion.30
  181.9 1.7 fusion.30
  204.3 1.7 fusion.30
  209.9 1.7 fusion.30
  215.5 1.7 fusion.30
  221.1 1.7 fusion.30
  226.7 1.7 fusion.30
  232.3 1.7 fusion.30
  237.9 1.7 fusion.30
  254.7 1.7 fusion.30
  260.2 1.7 fusion.30
  265.8 1.7 fusion.30
  271.4 1.7 fusion.30
  277.0 1.7 fusion.30
  282.6 1.7 fusion.30
  (507 shorter events, 272.0 us)
Async XLA Ops:
  30.3 42.9 %copy-start = (f32[2,3,768]{2,0,1:T(2,128)}, f32[2,3,768]{2,0,1:T(2,128)S(1)}, u32[]{:S(2)}) copy-start(f32[2,3,768]{2,0,1:T(2,128)S(1)} %fusion.8) | copy-start | bytes 55300
  32.1 41.2 %copy-start.1 = (f32[768]{0:T(1024)S(1)}, f32[768]{0:T(1024)}, u32[]{:S(2)}) copy-start(f32[768]{0:T(1024)} %param.7) | copy-start | bytes 9220
  32.1 40.3 %all-to-all-start = ((f32[32,2,4,768]{3,2,1,0:T(4,128)}), f32[32,2,4,768]{3,2,1,0:T(4,128)S(1)}, u32[]{:S(2)}, u32[]{:S(2)}) async-start(f32[32,2,4,768]{3,2,1,0:T(4,128)} %stack.2), calls=%async_computation | async-start | bytes 1572864 | tf_op jit(solution)/shard_map/all_to_all | solution.py:97
